TPU v7x, 32 devices: a whole 2x2x4 slice. The times are simulated.
32 devices in a mesh: expert: 4 (over x, core), hidden: 8 (over z, y).
Axes of the slice: x: 2, y: 2, z: 4, core: 2. Of those that a mesh axis runs over, the one named last changes fastest.
Arguments:
- tokens: bfloat16 [128, 6144], P(('expert', 'hidden')), may hold values from -33 to 33
- norm_gain: float32 [6144], replicated, may hold values from 0.1 to 1.9
- gate_weight: bfloat16 [4, 6144, 8192], P('expert', None, 'hidden'), may hold values from -0.078125 to 0.078125
- up_weight: bfloat16 [4, 6144, 8192], P('expert', None, 'hidden'), may hold values from -0.078125 to 0.078125
- down_weight: bfloat16 [4, 8192, 6144], P('expert', 'hidden'), may hold values from -0.09375 to 0.09375
- expert_ids: int32 [128, 2], P('expert'), may hold values from 0 to 3, all different within a row; in each aligned block of 4 rows (0 to 3, 4 to 7, ...) at most 2 rows name the same one
- route_weight: float32 [128, 2], P('expert'), may hold values from 0.2 to 1
Outputs:
- settled_state: bfloat16 [128, 6144], P(('expert', 'hidden'))
Inputs may be any that keep to these rules, and one draw needn't show every extreme that they name: `expert_ids`: in each aligned block of 4 rows (the tokens of one device) the two ids of a row differ and no expert is named more than 2 times; some expert is named exactly 2 times.
All inputs are finite; a program needn't handle non-finite values.
Results may differ from a plain program's by a relative error of at most 0.0085.
Values may be sent and summed in bfloat16 or wider, within the bound.
A program may use at most 64 MiB of HBM per device.

v0:
```python
import jax
import jax.numpy as jnp
from jax import lax
from jax.sharding import PartitionSpec as P

ITERS = 2


EPSILON = 1e-05
NUDGE = 0.5


def rms_norm(values, norm_gain):
    widened = values.astype(jnp.float32)
    mean_square = jnp.mean(widened * widened, axis=-1, keepdims=True)
    return (widened * lax.rsqrt(mean_square + EPSILON) * norm_gain).astype(jnp.bfloat16)


def slot_table(id_blocks, experts, capacity):
    groups = id_blocks.shape[0]
    tok_count = id_blocks.shape[1]
    flat_ids = id_blocks.reshape(groups, tok_count * 2)
    expert_range = jnp.arange(experts, dtype=jnp.int32)
    one_hot = (flat_ids[:, :, None] == expert_range[None, None, :]).astype(jnp.int32)
    before = jnp.cumsum(one_hot, axis=1) - one_hot
    within = jnp.sum(before * one_hot, axis=2)
    return (flat_ids * capacity + within).reshape(groups, tok_count, 2)


def dispatch(token_block, slots, slot_count):
    groups = token_block.shape[0]
    tok_count = token_block.shape[1]
    width = token_block.shape[2]
    token_index = jnp.broadcast_to(
        jnp.arange(tok_count, dtype=jnp.int32)[None, :, None], slots.shape
    )
    group_index = jnp.broadcast_to(jnp.arange(groups, dtype=jnp.int32)[:, None, None], slots.shape)
    source = (
        jnp.full((groups, slot_count), tok_count, jnp.int32).at[group_index, slots].set(token_index)
    )
    padded = jnp.concatenate(
        [token_block, jnp.zeros((groups, 1, width), token_block.dtype)], axis=1
    )
    return jax.vmap(lambda table_rows, chosen: jnp.take(table_rows, chosen, axis=0))(padded, source)


def expert_partial(inputs, gate_weight, up_weight, down_weight):
    gate_value = jnp.dot(inputs, gate_weight[0], preferred_element_type=jnp.float32)
    up_value = jnp.dot(inputs, up_weight[0], preferred_element_type=jnp.float32)
    hidden_units = (jax.nn.silu(gate_value) * up_value).astype(jnp.bfloat16)
    return jnp.dot(hidden_units, down_weight[0], preferred_element_type=jnp.float32)


def on_device(tokens, norm_gain, gate_weight, up_weight, down_weight, expert_ids, route_weight):
    experts = lax.axis_size("expert")
    tok_count = tokens.shape[0]
    capacity = tok_count // 2
    slot_count = experts * capacity
    position = lax.axis_index("hidden")
    own_ids = lax.dynamic_slice_in_dim(expert_ids, position * tok_count, tok_count, 0)
    own_weights = lax.dynamic_slice_in_dim(route_weight, position * tok_count, tok_count, 0)
    own_slots = slot_table(own_ids[None], experts, capacity)[0]
    state = tokens
    for iteration in range(ITERS):
        normed = rms_norm(state, norm_gain)
        outgoing = dispatch(normed[None], own_slots[None], slot_count)[0]
        arrived = lax.all_to_all(outgoing, "expert", split_axis=0, concat_axis=0, tiled=True)
        gathered = lax.all_gather(arrived, "hidden", axis=0, tiled=True)
        partials = expert_partial(gathered, gate_weight, up_weight, down_weight)
        summed = lax.psum_scatter(
            partials.astype(jnp.bfloat16), "hidden", scatter_dimension=0, tiled=True
        )
        returned = lax.all_to_all(summed, "expert", split_axis=0, concat_axis=0, tiled=True)
        first = (
            jnp.take(returned, own_slots[:, 0], axis=0).astype(jnp.float32) * own_weights[:, 0:1]
        )
        second = (
            jnp.take(returned, own_slots[:, 1], axis=0).astype(jnp.float32) * own_weights[:, 1:2]
        )
        mixed = first + second
        state = (
            NUDGE * state.astype(jnp.float32) + NUDGE * (tokens.astype(jnp.float32) + mixed)
        ).astype(jnp.bfloat16)
    return state


def solution(mesh):
    placed = (
        P(("expert", "hidden"), None),
        P(),
        P("expert", None, "hidden"),
        P("expert", None, "hidden"),
        P("expert", "hidden", None),
        P("expert", None),
        P("expert", None),
    )
    return jax.shard_map(
        on_device,
        mesh=mesh,
        in_specs=placed,
        out_specs=P(("expert", "hidden"), None),
        check_vma=False,
    )
```

profile of v0, /device:TPU:0, one launch (start us, length us, event | category | flops | bytes accessed | tf_op | source)
XLA Modules:
  0.0 285.9 jit_solution(7350800166975226673)
XLA Ops:
  6.5 0.7 copy-done
  7.3 0.1 copy.20
  7.5 0.2 reduce_window_sum.11
  7.8 0.1 copy.17
  7.9 0.1 copy.19
  8.2 0.6 scatter_custom_fusion
  8.8 1.0 fusion.51
  9.8 0.9 fusion.56
  10.7 0.8 gather_fusion
  11.7 8.3 %all_to_all.48 = bf16[4,2,6144]{2,1,0:T(2,128)(2,1)S(1)} all-to-all(bf16[4,2,6144]{2,1,0:T(2,128)(2,1)S(1)} %all_to_all.32), channel_id=1, replica_groups=mesh['expert'=4,'hidden'=8] {'expert'}, dimensions={0} | all-to-all | bytes 196608 | tf_op jit(solution)/shard_map/all_to_all | solution.py:67
  20.1 32.4 %all_gather.6 = bf16[64,6144]{1,0:T(8,128)(2,1)S(1)} all-gather(bf16[8,6144]{1,0:T(8,128)(2,1)S(1)} %all_to_all.34), channel_id=1, replica_groups=mesh['expert'=4,'hidden'=8] {'hidden'}, dimensions={0}, use_global_device_ids=true | all-gather | bytes 884736 | tf_op jit(solution)/shard_map/all_gather | solution.py:68
  52.5 6.9 %fusion.10 = f32[64,1024]{1,0:T(8,128)S(1)} fusion(bf16[64,6144]{1,0:T(8,128)(2,1)S(1)} %all_gather.6, bf16[1,6144,1024]{2,1,0:T(8,128)(2,1)} %param.13), kind=kOutput, calls=%fused_computation.17 | convolution fusion | flops 805306368 | bytes 13631488 | tf_op jit(solution)/shard_map/dot_general | solution.py:48
  59.5 13.6 %fusion.12 = bf16[64,6144]{1,0:T(8,128)(2,1)} fusion(bf16[1,1024,6144]{2,1,0:T(8,128)(2,1)} %param.15, bf16[64,6144]{1,0:T(8,128)(2,1)S(1)} %all_gather.6, bf16[1,6144,1024]{2,1,0:T(8,128)(2,1)} %param.14, f32[64,1024]{1,0:T(8,128)S(1)} %fusion.10), kind=kOutput, calls=%fused_computation.19 | convolution fusion | flops 1611399168 | bytes 27000832 | tf_op jit(solution)/shard_map/dot_general | solution.py:51
  73.2 0.2 slice_reduce_fusion.1
  73.4 63.1 %reduce-scatter.3.cloned.1.call-done = bf16[8,6144]{1,0:T(8,128)(2,1)} async-done(((bf16[64,6144]{1,0:T(8,128)(2,1)}), bf16[8,6144]{1,0:T(8,128)(2,1)}) %reduce-scatter.3.cloned.1.call-update) | async-done | bytes 98320 | tf_op jit(solution)/shard_map/reduce_scatter | solution.py:70
  136.5 1.6 all_to_all.35
  138.1 3.3 %all-to-all-start.1 = ((bf16[4,2,6144]{2,1,0:T(2,128)(2,1)}), bf16[4,2,6144]{2,1,0:T(2,128)(2,1)S(1)}, u32[]{:S(2)}, u32[]{:S(2)}) async-start(bf16[4,2,6144]{2,1,0:T(2,128)(2,1)} %all_to_all.35), calls=%async_computation.2 | async-start | bytes 196608 | tf_op jit(solution)/shard_map/all_to_all | solution.py:73
  141.5 4.2 %all-to-all-done.1 = bf16[4,2,6144]{2,1,0:T(2,128)(2,1)S(1)} async-done(((bf16[4,2,6144]{2,1,0:T(2,128)(2,1)}), bf16[4,2,6144]{2,1,0:T(2,128)(2,1)S(1)}, u32[]{:S(2)}, u32[]{:S(2)}) %all-to-all-start.1) | async-done | bytes 98336 | tf_op jit(solution)/shard_map/all_to_all | solution.py:73
  145.7 0.6 gather_fusion.2
  146.3 0.6 gather_fusion.1
  146.9 0.3 fusion.46
  147.3 0.8 gather_fusion.3
  148.3 6.7 %all_to_all.49 = bf16[4,2,6144]{2,1,0:T(2,128)(2,1)S(1)} all-to-all(bf16[4,2,6144]{2,1,0:T(2,128)(2,1)S(1)} %all_to_all.38), channel_id=1, replica_groups=mesh['expert'=4,'hidden'=8] {'expert'}, dimensions={0} | all-to-all | bytes 196608 | tf_op jit(solution)/shard_map/all_to_all | solution.py:67
  155.1 32.3 %all_gather.7 = bf16[64,6144]{1,0:T(8,128)(2,1)S(1)} all-gather(bf16[8,6144]{1,0:T(8,128)(2,1)S(1)} %all_to_all.40), channel_id=1, replica_groups=mesh['expert'=4,'hidden'=8] {'hidden'}, dimensions={0}, use_global_device_ids=true | all-gather | bytes 884736 | tf_op jit(solution)/shard_map/all_gather | solution.py:68
  187.3 6.9 %fusion.8 = f32[64,1024]{1,0:T(8,128)S(1)} fusion(bf16[64,6144]{1,0:T(8,128)(2,1)S(1)} %all_gather.7, bf16[1,6144,1024]{2,1,0:T(8,128)(2,1)} %param.13), kind=kOutput, calls=%fused_computation.15 | convolution fusion | flops 805306368 | bytes 13631488 | tf_op jit(solution)/shard_map/dot_general | solution.py:48
  194.2 13.6 %fusion.15 = bf16[64,6144]{1,0:T(8,128)(2,1)} fusion(bf16[1,1024,6144]{2,1,0:T(8,128)(2,1)} %param.15, bf16[64,6144]{1,0:T(8,128)(2,1)S(1)} %all_gather.7, bf16[1,6144,1024]{2,1,0:T(8,128)(2,1)} %param.14, f32[64,1024]{1,0:T(8,128)S(1)} %fusion.8), kind=kOutput, calls=%fused_computation.20 | convolution fusion | flops 1611399168 | bytes 27000832 | tf_op jit(solution)/shard_map/dot_general | solution.py:51
  207.8 61.5 %reduce-scatter.5.cloned.1.call-done = bf16[8,6144]{1,0:T(8,128)(2,1)} async-done(((bf16[64,6144]{1,0:T(8,128)(2,1)}), bf16[8,6144]{1,0:T(8,128)(2,1)}) %reduce-scatter.5.cloned.1.call-update) | async-done | bytes 98320 | tf_op jit(solution)/shard_map/reduce_scatter | solution.py:70
  269.3 1.0 all_to_all.41
  270.3 6.8 %all_to_all.50 = bf16[4,2,6144]{2,1,0:T(2,128)(2,1)S(1)} all-to-all(bf16[4,2,6144]{2,1,0:T(2,128)(2,1)S(1)} %all_to_all.41), channel_id=1, replica_groups=mesh['expert'=4,'hidden'=8] {'expert'}, dimensions={0} | all-to-all | bytes 196608 | tf_op jit(solution)/shard_map/all_to_all | solution.py:73
  277.1 0.6 gather_fusion.5
  277.7 0.6 gather_fusion.4
  278.3 0.8 fusion.50
  (45 shorter events, 1.3 us)
Async XLA Ops:
  6.5 0.7 copy-start
  6.5 130.0 %reduce-scatter.3.cloned.1.call-start = ((), (), s32[]{:S(2)}) async-start(), calls=%async_computation.6 | async-start | bytes 884736 | tf_op jit(solution)/shard_map/reduce_scatter | solution.py:70
  59.4 13.7 %copy-start.3 = (f32[32,2]{0,1:T(2,128)S(1)}, f32[32,2]{0,1:T(2,128)}, u32[]{:S(2)}) copy-start(f32[32,2]{0,1:T(2,128)} %param.17) | copy-start | bytes 772
  59.4 87.5 %copy-start.1 = (bf16[4,6144]{1,0:T(4,128)(2,1)S(1)}, bf16[4,6144]{1,0:T(4,128)(2,1)}, u32[]{:S(2)}) copy-start(bf16[4,6144]{1,0:T(4,128)(2,1)} %param.11) | copy-start | bytes 147460
  59.4 87.8 %copy-start.2 = (f32[6144]{0:T(1024)S(1)}, f32[6144]{0:T(1024)}, u32[]{:S(2)}) copy-start(f32[6144]{0:T(1024)} %param.12) | copy-start | bytes 73732
  138.1 7.6 %all-to-all-start.1 = ((bf16[4,2,6144]{2,1,0:T(2,128)(2,1)}), bf16[4,2,6144]{2,1,0:T(2,128)(2,1)S(1)}, u32[]{:S(2)}, u32[]{:S(2)}) async-start(bf16[4,2,6144]{2,1,0:T(2,128)(2,1)} %all_to_all.35), calls=%async_computation.2 | async-start | bytes 196608 | tf_op jit(solution)/shard_map/all_to_all | solution.py:73
  141.4 127.9 %reduce-scatter.5.cloned.1.call-start = ((), (), s32[]{:S(2)}) async-start(), calls=%async_computation.7 | async-start | bytes 884736 | tf_op jit(solution)/shard_map/reduce_scatter | solution.py:70
Sparse Core Ops, SparseCore 0:
  73.2 63.2 reduce-scatter.2
  207.9 61.2 reduce-scatter.4
where the time goes:
time: 286 us
  waiting for transfers between devices  129 us (45%)
  blocking collectives  86.4 us (30%)
  matrix products  40.9 us (14%)
  between operations  13.6 us (5%)
  local copies, waits for them, and re-layouts  9.26 us (3%)
  other arithmetic  3.46 us (1%)
  starting transfers between devices  3.35 us (1%)
    reduce_scatter x2, waiting for transfers between devices, on_device(): lax.psum_scatter(partials.astype(jnp.bfloat16), 'hidden', scatter_dimensi...  125 us
    all_gather x2, blocking collectives, on_device(): gathered = lax.all_gather(arrived, 'hidden', axis=0, tiled=True)  64.7 us
    dot_general x2, matrix products, expert_partial(): jnp.dot(hidden_units, down_weight[0], preferred_element_type=jnp.float32)  27.2 us
    all_to_all x2, blocking collectives, on_device(): lax.all_to_all(outgoing, 'expert', split_axis=0, concat_axis=0, tiled=True)  15 us
    dot_general x2, matrix products, expert_partial(): jnp.dot(inputs, gate_weight[0], preferred_element_type=jnp.float32)  13.8 us
    all_to_all x1, blocking collectives, on_device(): lax.all_to_all(summed, 'expert', split_axis=0, concat_axis=0, tiled=True)  6.77 us
  transfers between devices with their start and end apart: 3, of which 3 were waited for; matrix products, arithmetic and copies ran while one was open for 0% of the time, Pallas kernels for 0%

commit v1 on v0

v1 whole, which is shorter than its diff:
```python
import functools

import jax
import jax.numpy as jnp
from jax import lax
from jax.experimental import pallas as pl
from jax.experimental.pallas import tpu as pltpu
from jax.sharding import PartitionSpec as P

ITERS = 2
EPSILON = 1e-05
NUDGE = 0.5
CHUNKS = 4
LANES = 128
MESH = pl.DeviceIdType.MESH
f32, bf16 = jnp.float32, jnp.bfloat16


class Plan:
    def __init__(self, experts, hidden, tok, width, units):
        self.E, self.H, self.tok, self.D, self.U = experts, hidden, tok, width, units
        self.C = 2
        self.X = experts // self.C
        self.Y = 2
        self.Z = hidden // self.Y
        self.R = self.Z * tok
        self.NB = self.C * self.X * self.Y
        self.K = width // CHUNKS
        self.rows = self.NB * self.R
        self.numbers = {}

    def number(self, key):
        return self.numbers.setdefault(key, len(self.numbers))

    def block(self, rc, rx, ry):
        return (rc * self.X + rx) * self.Y + ry


def all_keys(p):
    for rc in range(p.C):
        for rx in range(p.X):
            if rc or rx:
                p.number(("route", rc, rx))
    for i in range(CHUNKS):
        for d in range(1, p.Z):
            p.number(("z", i, d))
        for b in range(1, p.NB):
            p.number(("blk", i, b))
        p.number(("core", i))
        f, s = (p.X, p.Y) if i % 2 == 0 else (p.Y, p.X)
        for d in range(1, f):
            p.number(("first", i, d))
        for d in range(1, s):
            p.number(("second", i, d))
        for d in range(1, p.Z):
            p.number(("back", i, d))


def tiles(count, body):
    if count == 1:
        body(0)
    else:
        pl.loop(0, count)(body)


def kernel(p, tokens_ref, gain_ref, route_ref, gate_hbm, up_hbm, down_hbm, out_ref,
           wg, wu, wd, xg, n4, z1, asm, acc, hid, route_in, wrow, state, keep, cs, cr,
           fs, fr, held, ss, sr, usum, own, bs, br, wsem, send_sem, recv_sem):
    C, X, Y, Z, R, K, T = p.C, p.X, p.Y, p.Z, p.R, p.K, p.tok
    e, h = lax.axis_index("expert"), lax.axis_index("hidden")
    x, c = e // C, e % C
    z, y = h // Y, h % Y

    def at(rc=0, rx=0, ry=0, rz=0):
        return ((x + rx) % X * C + (c + rc) % C, (z + rz) % Z * Y + (y + ry) % Y)

    loads = []
    for i in range(CHUNKS):
        rows = pl.ds(i * K, K)
        loads.append(pltpu.make_async_copy(gate_hbm.at[0, rows, :], wg.at[rows, :], wsem.at[3 * i]))
        loads.append(pltpu.make_async_copy(up_hbm.at[0, rows, :], wu.at[rows, :], wsem.at[3 * i + 1]))
    for i in range(CHUNKS):
        cols = pl.ds(i * K, K)
        loads.append(pltpu.make_async_copy(down_hbm.at[0, :, cols], wd.at[i], wsem.at[3 * i + 2]))
    for load in loads:
        load.start()

    barrier = pltpu.get_barrier_semaphore()
    partners = [at(rc=rc, rx=rx) for rc in range(C) for rx in range(X) if rc or rx]
    partners += [at(ry=d) for d in range(1, Y)] + [at(rz=d) for d in range(1, Z)]
    for partner in partners:
        pl.semaphore_signal(barrier, inc=1, device_id=partner, device_id_type=MESH)

    state[...] = tokens_ref[...].astype(f32)
    pl.semaphore_wait(barrier, len(partners))

    def copy(key, src, dst, to):
        n = p.number(key)
        return pltpu.make_async_remote_copy(
            src_ref=src, dst_ref=dst, send_sem=send_sem.at[n], recv_sem=recv_sem.at[n],
            device_id=to, device_id_type=MESH)

    def send(sent, *args):
        made = copy(*args)
        made.start()
        sent.append(made)

    def arrived(key, dst):
        copy(key, dst, dst, at(rc=1)).wait_recv()

    routes = []
    for rc in range(C):
        for rx in range(X):
            if rc or rx:
                send(routes, ("route", (-rc) % C, (-rx) % X), route_ref,
                     route_in.at[((-rc) % C) * X + (-rx) % X], at(rc=rc, rx=rx))

    def iteration(it, _):
        first_time = it == 0

        values = state[...]
        mean_square = jnp.sum(values * values, axis=-1, keepdims=True) / p.D
        normed = (values * lax.rsqrt(mean_square + EPSILON) * gain_ref[...]).astype(bf16)
        for i in range(CHUNKS):
            n4[i] = normed[:, i * K:(i + 1) * K]
        sent = []
        for i in range(CHUNKS):
            for d in range(1, Z):
                send(sent, ("z", i, Z - d), n4.at[i], z1.at[i, Z - d], at(rz=d))

        def block_to(i, b_from, rc, rx, ry):
            b, rest = b_from % Y, b_from // Y
            fx, fc = rest % X, rest // X
            there = p.block((fc - rc) % C, (fx - rx) % X, (b - ry) % Y)
            send(sent, ("blk", i, there), xg.at[i, b_from], xg.at[i, there], at(rc, rx, ry))

        def got(i, b):
            arrived(("blk", i, b), xg.at[i, b])

        def level1(i):
            for d in range(1, Z):
                arrived(("z", i, d), z1.at[i, d])
            asm[0:T, :] = n4[i].astype(f32)
            for d in range(1, Z):
                asm[d * T:(d + 1) * T, :] = z1[i, d].astype(f32)
            xg[i, 0] = asm[...].astype(bf16)
            for d in range(1, Y):
                block_to(i, 0, 0, 0, d)
            for d in range(1, X):
                block_to(i, 0, 0, d, 0)
            block_to(i, 0, 1, 0, 0)

        def level2(i):
            if i % 2 == 0:
                for ry in range(1, Y):
                    b = p.block(0, 0, ry)
                    got(i, b)
                    for d in range(1, X):
                        block_to(i, b, 0, d, 0)
                    block_to(i, b, 1, 0, 0)
                for rx in range(1, X):
                    b = p.block(0, rx, 0)
                    got(i, b)
                    block_to(i, b, 1, 0, 0)
            else:
                for rx in range(1, X):
                    b = p.block(0, rx, 0)
                    got(i, b)
                    for d in range(1, Y):
                        block_to(i, b, 0, 0, d)
                    block_to(i, b, 1, 0, 0)
                for ry in range(1, Y):
                    b = p.block(0, 0, ry)
                    got(i, b)
                    block_to(i, b, 1, 0, 0)

        def level3(i):
            for rx in range(1, X):
                for ry in range(1, Y):
                    b = p.block(0, rx, ry)
                    got(i, b)
                    block_to(i, b, 1, 0, 0)

        per = max(1, min(p.NB, 128 // R))
        row_tiles = p.NB // per
        high = per * R
        wide = min(512, p.U)

        def multiply(i):
            for b in range(X * Y, p.NB):
                got(i, b)

            @pl.when(first_time)
            def _():
                loads[2 * i].wait()
                loads[2 * i + 1].wait()

            def column(n):
                cols = pl.ds(pl.multiple_of(n * wide, wide), wide)

                def row(m):
                    block = xg[i, pl.ds(m * per, per)].reshape(high, K)
                    place = pl.ds(pl.multiple_of(m * high, high), high)
                    for side, weight in ((0, wg), (1, wu)):
                        product = jnp.dot(block, weight[pl.ds(i * K, K), cols], preferred_element_type=f32)
                        if i == 0:
                            acc[side, place, cols] = product
                        else:
                            acc[side, place, cols] += product

                tiles(row_tiles, row)

            tiles(p.U // wide, column)

        for t in range(CHUNKS + 3):
            if t < CHUNKS:
                level1(t)
            if 0 <= t - 1 < CHUNKS:
                level2(t - 1)
            if 0 <= t - 2 < CHUNKS:
                level3(t - 2)
            if 0 <= t - 3 < CHUNKS:
                multiply(t - 3)
        for made in sent:
            made.wait_send()

        @pl.when(first_time)
        def _():
            lane = lax.broadcasted_iota(jnp.int32, (T, LANES), 1)
            for rc in range(C):
                for rx in range(X):
                    if rc or rx:
                        arrived(("route", rc, rx), route_in.at[rc * X + rx])
                    for ry in range(Y):
                        for rz in range(Z):
                            _, whose = at(ry=ry, rz=rz)
                            if rc or rx:
                                part = route_in[rc * X + rx, whose]
                            else:
                                part = route_ref[whose]
                            mine = jnp.sum(jnp.where(lane == e, part, 0.0), axis=1, keepdims=True)
                            base = p.block(rc, rx, ry) * R + rz * T
                            wrow[base:base + T, :] = jnp.broadcast_to(mine, (T, LANES))

        def activate(n):
            cols = pl.ds(pl.multiple_of(n * LANES, LANES), LANES)

            def row(m):
                place = pl.ds(pl.multiple_of(m * high, high), high)
                gate = acc[0, place, cols]
                units = gate / (1.0 + jnp.exp(-gate)) * acc[1, place, cols]
                hid[place, cols] = (units * wrow[place, :]).astype(bf16)

            tiles(row_tiles, row)

        tiles(p.U // LANES, activate)

        sent = []
        half = p.rows // C
        narrow = 512 if K % 512 == 0 else LANES

        def down(i):
            @pl.when(first_time)
            def _():
                loads[2 * CHUNKS + i].wait()

            def column(n):
                cols = pl.ds(pl.multiple_of(n * narrow, narrow), narrow)

                def row(m):
                    place = pl.ds(pl.multiple_of(m * 64, 64), 64)
                    other = pl.ds(pl.multiple_of(half + m * 64, 64), 64)
                    cs[i, place, cols] = jnp.dot(hid[other, :], wd[i, :, cols], preferred_element_type=f32).astype(bf16)
                    keep[i % 2, place, cols] = jnp.dot(hid[place, :], wd[i, :, cols], preferred_element_type=f32)

                tiles(half // 64, row)

            tiles(K // narrow, column)
            send(sent, ("core", i), cs.at[i], cr.at[i], at(rc=1))

        def dims(i):
            if i % 2 == 0:
                return X, Y, lambda a, b: a * Y + b, lambda d: at(rx=d), lambda d: at(ry=d)
            return Y, X, lambda a, b: b * Y + a, lambda d: at(ry=d), lambda d: at(rx=d)

        def reduce1(i):
            arrived(("core", i), cr.at[i])
            F, S, place, to_first, _ = dims(i)
            for a in list(range(1, F)) + [0]:
                for b in range(S):
                    rows = pl.ds(place(a, b) * R, R)
                    total = keep[i % 2, rows, :] + cr[i, rows, :].astype(f32)
                    if a:
                        fs[i, (a - 1) * S + b] = total.astype(bf16)
                    else:
                        held[i % 2, b] = total
                if a:
                    send(sent, ("first", i, a), fs.at[i, pl.ds((a - 1) * S, S)],
                         fr.at[i, pl.ds((a - 1) * S, S)], to_first(a))

        def reduce2(i):
            F, S, _, _, to_second = dims(i)
            for a in range(1, F):
                arrived(("first", i, a), fr.at[i, pl.ds((a - 1) * S, S)])
            for b in list(range(1, S)) + [0]:
                total = held[i % 2, b]
                for a in range(1, F):
                    total = total + fr[i, (a - 1) * S + b].astype(f32)
                if b:
                    ss[i, b - 1] = total.astype(bf16)
                    send(sent, ("second", i, b), ss.at[i, b - 1], sr.at[i, b - 1], to_second(b))
                else:
                    usum[i % 2] = total

        def reduce3(i):
            S = dims(i)[1]
            total = usum[i % 2]
            for b in range(1, S):
                arrived(("second", i, b), sr.at[i, b - 1])
                total = total + sr[i, b - 1].astype(f32)
            asm[...] = total
            for d in range(1, Z):
                bs[i, d - 1] = asm[d * T:(d + 1) * T, :].astype(bf16)
                send(sent, ("back", i, d), bs.at[i, d - 1], br.at[i, d - 1], at(rz=d))
            own[i] = asm[0:T, :]

        def settle(i):
            mixed = own[i]
            for d in range(1, Z):
                arrived(("back", i, d), br.at[i, d - 1])
                mixed = mixed + br[i, d - 1].astype(f32)
            cols = pl.ds(i * K, K)
            fresh = (NUDGE * state[:, cols] + NUDGE * (tokens_ref[:, cols].astype(f32) + mixed)).astype(bf16)
            state[:, cols] = fresh.astype(f32)
            out_ref[:, cols] = fresh

        steps = (down, reduce1, reduce2, reduce3, settle)
        for t in range(CHUNKS + len(steps) - 1):
            for lag, step in enumerate(steps):
                if 0 <= t - lag < CHUNKS:
                    step(t - lag)
        for made in sent:
            made.wait_send()
        return 0

    lax.fori_loop(0, ITERS, iteration, 0)
    for made in routes:
        made.wait_send()


def on_device(experts, hidden, tokens, norm_gain, gate_weight, up_weight, down_weight, expert_ids, route_weight):
    tok, width = tokens.shape
    p = Plan(experts, hidden, tok, width, gate_weight.shape[2])
    all_keys(p)
    lanes = jnp.arange(LANES, dtype=jnp.int32)[None, :]
    table = (jnp.where(expert_ids[:, 0:1] == lanes, route_weight[:, 0:1], 0.0)
             + jnp.where(expert_ids[:, 1:2] == lanes, route_weight[:, 1:2], 0.0))
    table = table.reshape(hidden, tok, LANES)
    n, K, R, U = len(p.numbers), p.K, p.R, p.U
    S, FS = max(p.X, p.Y), max((p.X - 1) * p.Y, (p.Y - 1) * p.X)
    half = p.rows // p.C
    vmem = pltpu.VMEM
    scratch = [
        vmem((width, U), bf16), vmem((width, U), bf16), vmem((CHUNKS, U, K), bf16),
        vmem((CHUNKS, p.NB, R, K), bf16),
        vmem((CHUNKS, tok, K), bf16), vmem((CHUNKS, p.Z, tok, K), bf16), vmem((R, K), f32),
        vmem((2, p.rows, U), f32), vmem((p.rows, U), bf16),
        vmem((experts, hidden, tok, LANES), f32), vmem((p.rows, LANES), f32),
        vmem((tok, width), f32),
        vmem((2, half, K), f32), vmem((CHUNKS, half, K), bf16), vmem((CHUNKS, half, K), bf16),
        vmem((CHUNKS, FS, R, K), bf16), vmem((CHUNKS, FS, R, K), bf16),
        vmem((2, S, R, K), f32),
        vmem((CHUNKS, S - 1, R, K), bf16), vmem((CHUNKS, S - 1, R, K), bf16),
        vmem((2, R, K), f32),
        vmem((CHUNKS, tok, K), f32),
        vmem((CHUNKS, p.Z - 1, tok, K), bf16), vmem((CHUNKS, p.Z - 1, tok, K), bf16),
        pltpu.SemaphoreType.DMA((3 * CHUNKS,)),
        pltpu.SemaphoreType.DMA((n,)), pltpu.SemaphoreType.DMA((n,)),
    ]
    inside = pl.BlockSpec(memory_space=pltpu.VMEM)
    outside = pl.BlockSpec(memory_space=pl.ANY)
    return pl.pallas_call(
        functools.partial(kernel, p),
        out_shape=jax.ShapeDtypeStruct((tok, width), bf16),
        in_specs=[inside] * 3 + [outside] * 3,
        out_specs=inside,
        scratch_shapes=scratch,
        compiler_params=pltpu.CompilerParams(
            collective_id=0, has_side_effects=True, vmem_limit_bytes=67_000_000),
        name="settle",
    )(tokens, norm_gain.reshape(1, width), table, gate_weight, up_weight, down_weight)


def solution(mesh):
    placed = (
        P(("expert", "hidden"), None),
        P(),
        P("expert", None, "hidden"),
        P("expert", None, "hidden"),
        P("expert", "hidden", None),
        P("expert", None),
        P("expert", None),
    )
    return jax.shard_map(
        functools.partial(on_device, mesh.shape["expert"], mesh.shape["hidden"]),
        mesh=mesh,
        in_specs=placed,
        out_specs=P(("expert", "hidden"), None),
        check_vma=False,
    )
```

time: 286 us -> 94.3 us (0.33)
  waiting for transfers between devices: 129 us -> 0 us
  Pallas kernels: 0 us -> 90 us
  blocking collectives: 86.4 us -> 0 us
  matrix products: 40.9 us -> 0 us
  between operations: 13.6 us -> 0.01 us
  local copies, waits for them, and re-layouts: 9.26 us -> 3.29 us
  starting transfers between devices: 3.35 us -> 0 us
    reduce_scatter x2 -> x0, waiting for transfers between devices: 125 us -> none  [on_device(): lax.psum_scatter(partials.astype(jnp.bfloat16), 'hidden', scatter_dimensi...]
    pallas_call x0 -> x1, Pallas kernels: none -> 90 us  [on_device(): pl.pallas_call(functools.partial(kernel, p), out_shape=jax.ShapeDtypeStru...]
    all_gather x2 -> x0, blocking collectives: 64.7 us -> none  [on_device(): gathered = lax.all_gather(arrived, 'hidden', axis=0, tiled=True)]
    dot_general x4 -> x0, matrix products: 40.9 us -> none  [the longest x2 27.2 us: expert_partial(): jnp.dot(hidden_units, down_weight[0], preferred_element_type=jnp.float32)]
    all_to_all x3 -> x0, blocking collectives: 21.8 us -> none  [the longest x2 15 us: on_device(): lax.all_to_all(outgoing, 'expert', split_axis=0, concat_axis=0, tiled=True)]
    all_to_all x1 -> x0, waiting for transfers between devices: 4.2 us -> none  [on_device(): lax.all_to_all(summed, 'expert', split_axis=0, concat_axis=0, tiled=True)]
    gather x7 -> x0, local copies, waits for them, and re-layouts: 4.06 us -> none  [the longest x3 1.68 us: dispatch(): jnp.take(table_rows, chosen, axis=0)]
    all_to_all x1 -> x0, starting transfers between devices: 3.3 us -> none  [on_device(): lax.all_to_all(summed, 'expert', split_axis=0, concat_axis=0, tiled=True)]
  transfers between devices with their start and end apart: 3 -> 0, of which waited for: 3 -> 0; matrix products, arithmetic and copies ran while one was open for 0% -> 0% of each run, Pallas kernels for 0% -> 0%
where the time goes in v1:
time: 94.3 us; the launch traced here: 94 us
  Pallas kernels  90 us (95%)
  local copies, waits for them, and re-layouts  3.29 us (3%)
    pallas_call x1, Pallas kernels, on_device(): pl.pallas_call(functools.partial(kernel, p), out_shape=jax.ShapeDtypeStru...  90 us

profile of v1, /device:TPU:0, one launch (start us, length us, event | category | flops | bytes accessed | tf_op | source)
XLA Modules:
  0.0 94.0 jit_solution(15800175964575195577)
XLA Ops:
  0.0 0.8 slice_reduce_fusion.3
  0.8 0.8 slice_reduce_fusion.2
  1.5 0.1 broadcast_in_dim.23
  1.6 0.1 eq.32
  1.7 0.1 broadcast_in_dim.26
  1.8 0.1 eq.36
  1.9 0.7 select_add_fusion.route_ref
  2.6 90.0 %settle.1 = bf16[4,6144]{1,0:T(4,128)(2,1)} custom-call(bf16[4,6144]{1,0:T(4,128)(2,1)} %tokens_ref.1, f32[1,6144]{1,0:T(1,128)} %bitcast.1, f32[8,4,128]{2,1,0:T(4,128)} %select_add_fusion.route_ref, bf16[1,6144,1024]{2,1,0:T(8,128)(2,1)} %gate_hbm.1, bf16[1,6144,1024]{2,1,0:T(8,128)(2,1)} %up_hbm.1, bf16[1,1024,6144]{2,1,0:T(8,128)(2,1)} %down_hbm.1), custom_call_target="tpu_custom_call" | custom-call | tf_op jit(solution)/shard_map/settle/pallas_call | solution.py:382
  92.6 1.4 %copy.9 = bf16[4,6144]{1,0:T(4,128)(2,1)} copy(bf16[4,6144]{1,0:T(4,128)(2,1)} %settle.1) | data formatting | bytes 98304

commit v2 on v1

--- a/solution.py
+++ b/solution.py
@@ -10,7 +10,7 @@
 ITERS = 2
 EPSILON = 1e-05
 NUDGE = 0.5
-CHUNKS = 4
+CHUNKS = 6
 LANES = 128
 MESH = pl.DeviceIdType.MESH
 f32, bf16 = jnp.float32, jnp.bfloat16
@@ -65,7 +65,7 @@
 
 def kernel(p, tokens_ref, gain_ref, route_ref, gate_hbm, up_hbm, down_hbm, out_ref,
            wg, wu, wd, xg, n4, z1, asm, acc, hid, route_in, wrow, state, keep, cs, cr,
-           fs, fr, held, ss, sr, usum, own, bs, br, wsem, send_sem, recv_sem):
+           fs, fr, held, ss, sr, usum, own, bs, br, scaled, square, wsem, send_sem, recv_sem):
     C, X, Y, Z, R, K, T = p.C, p.X, p.Y, p.Z, p.R, p.K, p.tok
     e, h = lax.axis_index("expert"), lax.axis_index("hidden")
     x, c = e // C, e % C
@@ -92,6 +92,8 @@
         pl.semaphore_signal(barrier, inc=1, device_id=partner, device_id_type=MESH)
 
     state[...] = tokens_ref[...].astype(f32)
+    for i in range(CHUNKS):
+        n4[i] = tokens_ref[:, i * K:(i + 1) * K]
     pl.semaphore_wait(barrier, len(partners))
 
     def copy(key, src, dst, to):
@@ -115,24 +117,24 @@
                 send(routes, ("route", (-rc) % C, (-rx) % X), route_ref,
                      route_in.at[((-rc) % C) * X + (-rx) % X], at(rc=rc, rx=rx))
 
-    def iteration(it, _):
-        first_time = it == 0
-
-        values = state[...]
-        mean_square = jnp.sum(values * values, axis=-1, keepdims=True) / p.D
-        normed = (values * lax.rsqrt(mean_square + EPSILON) * gain_ref[...]).astype(bf16)
-        for i in range(CHUNKS):
-            n4[i] = normed[:, i * K:(i + 1) * K]
-        sent = []
-        for i in range(CHUNKS):
-            for d in range(1, Z):
-                send(sent, ("z", i, Z - d), n4.at[i], z1.at[i, Z - d], at(rz=d))
-
+    gathers, sums = [], []
+
+    def spread(i):
+        for d in range(1, Z):
+            send(gathers, ("z", i, Z - d), n4.at[i], z1.at[i, Z - d], at(rz=d))
+
+    def settle_sends():
+        for made in gathers + sums:
+            made.wait_send()
+        gathers.clear()
+        sums.clear()
+
+    def gather_steps(it):
         def block_to(i, b_from, rc, rx, ry):
             b, rest = b_from % Y, b_from // Y
             fx, fc = rest % X, rest // X
             there = p.block((fc - rc) % C, (fx - rx) % X, (b - ry) % Y)
-            send(sent, ("blk", i, there), xg.at[i, b_from], xg.at[i, there], at(rc, rx, ry))
+            send(gathers, ("blk", i, there), xg.at[i, b_from], xg.at[i, there], at(rc, rx, ry))
 
         def got(i, b):
             arrived(("blk", i, b), xg.at[i, b])
@@ -181,51 +183,57 @@
                     got(i, b)
                     block_to(i, b, 1, 0, 0)
 
-        per = max(1, min(p.NB, 128 // R))
-        row_tiles = p.NB // per
-        high = per * R
-        wide = min(512, p.U)
-
         def multiply(i):
             for b in range(X * Y, p.NB):
                 got(i, b)
 
-            @pl.when(first_time)
-            def _():
+            if it == 0:
                 loads[2 * i].wait()
                 loads[2 * i + 1].wait()
 
-            def column(n):
-                cols = pl.ds(pl.multiple_of(n * wide, wide), wide)
-
-                def row(m):
-                    block = xg[i, pl.ds(m * per, per)].reshape(high, K)
-                    place = pl.ds(pl.multiple_of(m * high, high), high)
+            def row(m):
+                place = pl.ds(pl.multiple_of(m * high, high), high)
+
+                def prepare(n):
+                    cols = pl.ds(pl.multiple_of(n * LANES, LANES), LANES)
+                    gains = gain_ref[:, pl.ds(pl.multiple_of(i * K + n * LANES, LANES), LANES)]
+                    part = xg[i, pl.ds(m * per, per), :, cols].reshape(high, LANES).astype(f32)
+                    scaled[:, cols] = (part * gains).astype(bf16)
+                    if i == 0:
+                        @pl.when(n == 0)
+                        def _():
+                            square[place, :] = part * part
+
+                        @pl.when(n > 0)
+                        def _():
+                            square[place, :] += part * part
+                    else:
+                        square[place, :] += part * part
+
+                tiles(K // LANES, prepare)
+
+                def column(n):
+                    cols = pl.ds(pl.multiple_of(n * wide, wide), wide)
                     for side, weight in ((0, wg), (1, wu)):
-                        product = jnp.dot(block, weight[pl.ds(i * K, K), cols], preferred_element_type=f32)
+                        product = jnp.dot(scaled[...], weight[pl.ds(i * K, K), cols], preferred_element_type=f32)
                         if i == 0:
                             acc[side, place, cols] = product
                         else:
                             acc[side, place, cols] += product
 
-                tiles(row_tiles, row)
-
-            tiles(p.U // wide, column)
-
-        for t in range(CHUNKS + 3):
-            if t < CHUNKS:
-                level1(t)
-            if 0 <= t - 1 < CHUNKS:
-                level2(t - 1)
-            if 0 <= t - 2 < CHUNKS:
-                level3(t - 2)
-            if 0 <= t - 3 < CHUNKS:
-                multiply(t - 3)
-        for made in sent:
-            made.wait_send()
-
-        @pl.when(first_time)
-        def _():
+                tiles(p.U // wide, column)
+
+            tiles(row_tiles, row)
+
+        return level1, level2, level3, multiply
+
+    per = max(1, min(p.NB, 128 // R))
+    row_tiles = p.NB // per
+    high = per * R
+    wide = min(512, p.U)
+
+    def read_routes():
+        if True:
             lane = lax.broadcasted_iota(jnp.int32, (T, LANES), 1)
             for rc in range(C):
                 for rx in range(X):
@@ -242,26 +250,34 @@
                             base = p.block(rc, rx, ry) * R + rz * T
                             wrow[base:base + T, :] = jnp.broadcast_to(mine, (T, LANES))
 
+    def activate_all():
+        def root(m):
+            place = pl.ds(pl.multiple_of(m * high, high), high)
+            mean_square = jnp.sum(square[place, :], axis=1, keepdims=True) / p.D
+            square[place, :] = jnp.broadcast_to(lax.rsqrt(mean_square + EPSILON), (high, LANES))
+
+        tiles(row_tiles, root)
+
         def activate(n):
             cols = pl.ds(pl.multiple_of(n * LANES, LANES), LANES)
 
             def row(m):
                 place = pl.ds(pl.multiple_of(m * high, high), high)
-                gate = acc[0, place, cols]
-                units = gate / (1.0 + jnp.exp(-gate)) * acc[1, place, cols]
+                scale = square[place, :]
+                gate = acc[0, place, cols] * scale
+                units = gate / (1.0 + jnp.exp(-gate)) * (acc[1, place, cols] * scale)
                 hid[place, cols] = (units * wrow[place, :]).astype(bf16)
 
             tiles(row_tiles, row)
 
         tiles(p.U // LANES, activate)
 
-        sent = []
+    def sum_steps(it):
         half = p.rows // C
         narrow = 512 if K % 512 == 0 else LANES
 
         def down(i):
-            @pl.when(first_time)
-            def _():
+            if it == 0:
                 loads[2 * CHUNKS + i].wait()
 
             def column(n):
@@ -276,7 +292,7 @@
                 tiles(half // 64, row)
 
             tiles(K // narrow, column)
-            send(sent, ("core", i), cs.at[i], cr.at[i], at(rc=1))
+            send(sums, ("core", i), cs.at[i], cr.at[i], at(rc=1))
 
         def dims(i):
             if i % 2 == 0:
@@ -295,7 +311,7 @@
                     else:
                         held[i % 2, b] = total
                 if a:
-                    send(sent, ("first", i, a), fs.at[i, pl.ds((a - 1) * S, S)],
+                    send(sums, ("first", i, a), fs.at[i, pl.ds((a - 1) * S, S)],
                          fr.at[i, pl.ds((a - 1) * S, S)], to_first(a))
 
         def reduce2(i):
@@ -308,7 +324,7 @@
                     total = total + fr[i, (a - 1) * S + b].astype(f32)
                 if b:
                     ss[i, b - 1] = total.astype(bf16)
-                    send(sent, ("second", i, b), ss.at[i, b - 1], sr.at[i, b - 1], to_second(b))
+                    send(sums, ("second", i, b), ss.at[i, b - 1], sr.at[i, b - 1], to_second(b))
                 else:
                     usum[i % 2] = total
 
@@ -321,7 +337,7 @@
             asm[...] = total
             for d in range(1, Z):
                 bs[i, d - 1] = asm[d * T:(d + 1) * T, :].astype(bf16)
-                send(sent, ("back", i, d), bs.at[i, d - 1], br.at[i, d - 1], at(rz=d))
+                send(sums, ("back", i, d), bs.at[i, d - 1], br.at[i, d - 1], at(rz=d))
             own[i] = asm[0:T, :]
 
         def settle(i):
@@ -332,18 +348,32 @@
             cols = pl.ds(i * K, K)
             fresh = (NUDGE * state[:, cols] + NUDGE * (tokens_ref[:, cols].astype(f32) + mixed)).astype(bf16)
             state[:, cols] = fresh.astype(f32)
-            out_ref[:, cols] = fresh
-
-        steps = (down, reduce1, reduce2, reduce3, settle)
-        for t in range(CHUNKS + len(steps) - 1):
-            for lag, step in enumerate(steps):
+            if it == ITERS - 1:
+                out_ref[:, cols] = fresh
+            else:
+                n4[i] = fresh
+                spread(i)
+
+        return down, reduce1, reduce2, reduce3, settle
+
+    def staggered(steps):
+        for t in range(CHUNKS + max(lag for lag, _ in steps)):
+            for lag, step in steps:
                 if 0 <= t - lag < CHUNKS:
                     step(t - lag)
-        for made in sent:
-            made.wait_send()
-        return 0
-
-    lax.fori_loop(0, ITERS, iteration, 0)
+
+    for i in range(CHUNKS):
+        spread(i)
+    staggered(list(enumerate(gather_steps(0))))
+    read_routes()
+    for it in range(ITERS):
+        settle_sends()
+        activate_all()
+        steps = list(enumerate(sum_steps(it)))
+        if it < ITERS - 1:
+            steps += [(6 + lag, step) for lag, step in enumerate(gather_steps(it + 1))]
+        staggered(steps)
+    settle_sends()
     for made in routes:
         made.wait_send()
 
@@ -353,8 +383,7 @@
     p = Plan(experts, hidden, tok, width, gate_weight.shape[2])
     all_keys(p)
     lanes = jnp.arange(LANES, dtype=jnp.int32)[None, :]
-    table = (jnp.where(expert_ids[:, 0:1] == lanes, route_weight[:, 0:1], 0.0)
-             + jnp.where(expert_ids[:, 1:2] == lanes, route_weight[:, 1:2], 0.0))
+    table = jnp.sum(jnp.where(expert_ids[:, :, None] == lanes[None], route_weight[:, :, None], 0.0), axis=1)
     table = table.reshape(hidden, tok, LANES)
     n, K, R, U = len(p.numbers), p.K, p.R, p.U
     S, FS = max(p.X, p.Y), max((p.X - 1) * p.Y, (p.Y - 1) * p.X)
@@ -374,6 +403,7 @@
         vmem((2, R, K), f32),
         vmem((CHUNKS, tok, K), f32),
         vmem((CHUNKS, p.Z - 1, tok, K), bf16), vmem((CHUNKS, p.Z - 1, tok, K), bf16),
+        vmem((max(1, min(p.NB, 128 // R)) * R, K), bf16), vmem((p.rows, LANES), f32),
         pltpu.SemaphoreType.DMA((3 * CHUNKS,)),
         pltpu.SemaphoreType.DMA((n,)), pltpu.SemaphoreType.DMA((n,)),
     ]

time: 94.3 us -> 98.5 us (1.045)
  Pallas kernels: 90 us -> 95.4 us
  local copies, waits for them, and re-layouts: 3.29 us -> 1.44 us
    pallas_call x1, Pallas kernels: 90 us -> 95.4 us  [on_device(): pl.pallas_call(functools.partial(kernel, p), out_shape=jax.ShapeDtypeStru...]
    slice x2 -> x0, local copies, waits for them, and re-layouts: 1.54 us -> none  [the longest x1 0.77 us: on_device(): route_weight[:, 0:1]]
    reduce_sum x0 -> x1, other arithmetic: none -> 1.39 us  [on_device(): jnp.sum(jnp.where(expert_ids[:, :, None] == lanes[None], route_weight[:,...]
where the time goes in v2:
time: 98.5 us; the launch traced here: 98.3 us
  Pallas kernels  95.4 us (97%)
  local copies, waits for them, and re-layouts  1.44 us (1%)
  other arithmetic  1.39 us (1%)
    pallas_call x1, Pallas kernels, on_device(): pl.pallas_call(functools.partial(kernel, p), out_shape=jax.ShapeDtypeStru...  95.4 us

profile of v2, /device:TPU:0, one launch (start us, length us, event | category | flops | bytes accessed | tf_op | source)
XLA Modules:
  0.0 98.3 jit_solution(5156308057252459316)
XLA Ops:
  0.0 1.4 %select_reduce_fusion = f32[32,128]{1,0:T(8,128)} fusion(f32[32,2]{0,1:T(2,128)} %param.13, s32[32,2]{0,1:T(2,128)} %param.12), kind=kLoop, calls=%fused_computation | loop fusion | flops 20480 | bytes 16896 | tf_op jit(solution)/shard_map/reduce_sum | solution.py:386
  1.4 95.4 %settle.1 = bf16[4,6144]{1,0:T(4,128)(2,1)} custom-call(bf16[4,6144]{1,0:T(4,128)(2,1)} %tokens_ref.1, f32[1,6144]{1,0:T(1,128)} %bitcast.3, f32[8,4,128]{2,1,0:T(4,128)} %bitcast.2, bf16[1,6144,1024]{2,1,0:T(8,128)(2,1)} %gate_hbm.1, bf16[1,6144,1024]{2,1,0:T(8,128)(2,1)} %up_hbm.1, bf16[1,1024,6144]{2,1,0:T(8,128)(2,1)} %down_hbm.1), custom_call_target="tpu_custom_call" | custom-call | tf_op jit(solution)/shard_map/settle/pallas_call | solution.py:412
  96.8 1.4 %copy.11 = bf16[4,6144]{1,0:T(4,128)(2,1)} copy(bf16[4,6144]{1,0:T(4,128)(2,1)} %settle.1) | data formatting | bytes 98304
